TPU v7x, 128 devices: a whole 4x4x4 slice. The times are simulated.
128 devices in a mesh: dp: 8 (over y, core), ctx: 16 (over z, x).
Axes of the slice: x: 4, y: 4, z: 4, core: 2. Of those that a mesh axis runs over, the one named last changes fastest.
Arguments:
- queries: bfloat16 [8, 4096, 256], P('dp', 'ctx'), may hold values from -6 to 6
- keys: bfloat16 [8, 4096, 256], P('dp', 'ctx'), may hold values from -6 to 6
- values: bfloat16 [8, 4096, 256], P('dp', 'ctx'), may hold values from -6 to 6
- grad_out: bfloat16 [8, 4096, 256], P('dp', 'ctx'), may hold values from -6 to 6
- log_norm: float32 [8, 2, 4096], P('dp', None, 'ctx'), may hold values from 5 to 7
- offsets: int32 [2, 5], replicated, may hold values from 0 to 15
- q_gain: float32 [256], replicated, may hold values from 0.5 to 2
Outputs:
- grad_queries: bfloat16 [8, 4096, 256], P('dp', 'ctx')
- grad_keys: bfloat16 [8, 4096, 256], P('dp', 'ctx')
- grad_values: bfloat16 [8, 4096, 256], P('dp', 'ctx')
- grad_gain: float32 [256], replicated
All inputs are finite; a program needn't handle non-finite values.
Results may differ from a plain program's by a relative error of at most 0.013.
The roundings to bfloat16 on the way count: a program that leaves them out, or rounds other values in their place, can miss the bound.
Values may be sent and summed in bfloat16 or wider, within the bound.
No kernel may reach another device: no remote copies, remote signals or barrier semaphores. Data moves between devices by JAX's collectives and lax.ppermute only.
A program may use at most 64 MiB of HBM per device.

v0:
```python
import math
import jax
import jax.numpy as jnp
from jax import lax
from jax.sharding import PartitionSpec as P

BLOCK = 128
LEVELS = 5


def swapped(block, axis, stride):
    count = lax.axis_size(axis)
    route = []
    for low in range(count):
        high = low | 1 << stride
        if high != low and high < count:
            route += [(low, high), (high, low)]
    return lax.ppermute(block, axis, route)


def slot_table(device_local, offset_vec, stride, block_count):
    slot_count = (block_count + stride - 1) // stride
    base_block = device_local * block_count + jnp.zeros_like(offset_vec)
    first_step = jnp.maximum((base_block - offset_vec + stride - 1) // stride, 0)
    step_index = first_step[..., None] + jnp.arange(slot_count, dtype=jnp.int32)
    global_block = offset_vec[..., None] + stride * step_index
    local_block = global_block - base_block[..., None]
    usable = (step_index < block_count) & (local_block >= 0) & (local_block < block_count)
    return (jnp.clip(local_block, 0, block_count - 1), usable.astype(jnp.float32))


def segment_slots(shift_vec, span_len, block_count):
    device_col = jnp.arange(span_len, dtype=jnp.int32)[:, None]
    seg_block, seg_usable = slot_table(device_col, shift_vec[None, :], span_len, block_count)
    return (seg_block.transpose(1, 0, 2), seg_usable.transpose(1, 0, 2))


def select_table(local_block, block_count):
    return (local_block[..., None] == jnp.arange(block_count, dtype=jnp.int32)).astype(jnp.float32)


def pick_blocks(data, table):
    head_count, block_count = (data.shape[0], data.shape[1])
    flat = data.reshape(head_count, block_count, -1).astype(jnp.float32)
    chosen = jnp.einsum(
        "hsb,hbx->hsx",
        table,
        flat,
        precision=lax.Precision.HIGHEST,
        preferred_element_type=jnp.float32,
    ).astype(data.dtype)
    return chosen.reshape((head_count, -1) + data.shape[3:])


def place_rows(accum, contrib, table, usable):
    head_count, block_count = (accum.shape[0], accum.shape[1])
    slot_count = table.shape[1]
    weights = table * usable[..., None]
    shaped = contrib.reshape(head_count, slot_count, -1)
    added = jnp.einsum(
        "hsb,hsx->hbx",
        weights,
        shaped,
        precision=lax.Precision.HIGHEST,
        preferred_element_type=jnp.float32,
    )
    return accum + added.reshape(accum.shape)


def attend(
    query_rows,
    dout_rows,
    norm_rows,
    query_mask,
    key_rows,
    value_rows,
    key_mask,
    score_scale,
    row_block,
):
    head_count, query_count, head_dim = query_rows.shape
    steps = query_count // row_block

    def split(array):
        return jnp.moveaxis(array.reshape((head_count, steps, row_block) + array.shape[2:]), 1, 0)

    def step_fn(carry, parts):
        query_blk, dout_blk, norm_blk, mask_blk = parts
        scores = (
            jnp.einsum("hqd,hkd->hqk", query_blk, key_rows, preferred_element_type=jnp.float32)
            * score_scale
        )
        probs = jnp.exp(scores - norm_blk[:, :, None]) * mask_blk[:, :, None] * key_mask[:, None, :]
        probs_low = probs.astype(jnp.bfloat16)
        prob_grad = jnp.einsum(
            "hqd,hkd->hqk", dout_blk, value_rows, preferred_element_type=jnp.float32
        )
        dscore = (probs * prob_grad).astype(jnp.bfloat16)
        query_grad = (
            jnp.einsum("hqk,hkd->hqd", dscore, key_rows, preferred_element_type=jnp.float32)
            * score_scale
        )
        key_part = (
            jnp.einsum("hqk,hqd->hkd", dscore, query_blk, preferred_element_type=jnp.float32)
            * score_scale
        )
        value_part = jnp.einsum(
            "hqk,hqd->hkd", probs_low, dout_blk, preferred_element_type=jnp.float32
        )
        return ((carry[0] + key_part, carry[1] + value_part), query_grad)

    start = jnp.zeros((head_count, key_rows.shape[1], head_dim), jnp.float32)
    totals, query_parts = lax.scan(
        step_fn,
        (start, start),
        (split(query_rows), split(dout_rows), split(norm_rows), split(query_mask)),
    )
    query_grad = jnp.moveaxis(query_parts, 0, 1).reshape(head_count, query_count, head_dim)
    return (query_grad, totals[0], totals[1])


def swap_up(payload, my_index, bit_total):
    for bit_idx in range(bit_total):
        partner = swapped(payload, "ctx", bit_idx)
        lower_half = my_index >> bit_idx & 1 == 0
        payload = jnp.where(
            lower_half,
            jnp.concatenate([payload, partner], axis=1),
            jnp.concatenate([partner, payload], axis=1),
        )
    return payload


def swap_down(sums_kv, my_index, bit_total):
    head_count = sums_kv.shape[0]
    for bit_idx in reversed(range(bit_total)):
        halves = sums_kv.reshape(head_count, 2, -1, sums_kv.shape[-1])
        lower_half = my_index >> bit_idx & 1 == 0
        kept_half = jnp.where(lower_half, halves[:, 0], halves[:, 1])
        sent_half = jnp.where(lower_half, halves[:, 1], halves[:, 0])
        sums_kv = kept_half + swapped(sent_half.astype(jnp.bfloat16), "ctx", bit_idx).astype(
            sent_half.dtype
        )
    return sums_kv


def body(queries, keys, values, grad_out, log_norm, offsets, q_gain):
    query_raw = queries[0]
    token_count, proj_width = query_raw.shape
    head_count = log_norm.shape[1]
    head_dim = proj_width // head_count
    block_count = token_count // BLOCK
    ctx_size = lax.axis_size("ctx")
    score_scale = head_dim ** (-0.5)
    scaled = (query_raw.astype(jnp.float32) * q_gain).astype(jnp.bfloat16)

    def heads(matrix):
        return (
            matrix.reshape(token_count, head_count, head_dim)
            .transpose(1, 0, 2)
            .reshape(head_count, block_count, BLOCK, head_dim)
        )

    query_all = heads(scaled)
    key_all = heads(keys[0])
    value_all = heads(values[0])
    dout_all = heads(grad_out[0])
    norm_all = log_norm[0].reshape(head_count, block_count, BLOCK)
    query_acc = jnp.zeros((head_count, block_count, BLOCK, head_dim), jnp.float32)
    kv_acc = jnp.zeros((head_count, block_count, BLOCK, 2 * head_dim), jnp.float32)
    my_index = lax.axis_index("ctx")
    for level_idx in range(LEVELS):
        span_len = min(2**level_idx, ctx_size)
        shift_vec = offsets[:, level_idx] % span_len
        local_block, usable = slot_table(my_index % span_len, shift_vec, span_len, block_count)
        table = select_table(local_block, block_count)
        slot_count = local_block.shape[1]
        row_block = BLOCK * math.gcd(slot_count, max(1, 512 // BLOCK))
        query_own = pick_blocks(query_all, table)
        dout_own = pick_blocks(dout_all, table)
        norm_own = pick_blocks(norm_all, table)
        mask_own = jnp.repeat(usable, BLOCK, axis=1)
        payload = jnp.concatenate(
            [pick_blocks(key_all, table), pick_blocks(value_all, table)], axis=2
        )
        bit_total = span_len.bit_length() - 1
        payload = swap_up(payload, my_index, bit_total)
        seg_block, seg_usable = segment_slots(shift_vec, span_len, block_count)
        seg_mask = jnp.repeat(seg_usable.reshape(head_count, -1), BLOCK, axis=1)
        level_query, level_key, level_value = attend(
            query_own,
            dout_own,
            norm_own,
            mask_own,
            payload[..., :head_dim],
            payload[..., head_dim:],
            seg_mask,
            score_scale,
            row_block,
        )
        sums_kv = jnp.concatenate([level_key, level_value], axis=2)
        sums_kv = swap_down(sums_kv, my_index, bit_total)
        query_acc = place_rows(query_acc, level_query, table, usable)
        kv_acc = place_rows(kv_acc, sums_kv, table, usable)

    def to_rows(field_acc):
        return (
            field_acc.reshape(head_count, token_count, -1)
            .transpose(1, 0, 2)
            .reshape(token_count, -1)
        )

    dq_rows = to_rows(query_acc)
    grad_queries = (dq_rows * q_gain).astype(jnp.bfloat16)
    grad_keys = to_rows(kv_acc[..., :head_dim]).astype(jnp.bfloat16)
    grad_values = to_rows(kv_acc[..., head_dim:]).astype(jnp.bfloat16)
    gain_total = lax.psum(jnp.sum(query_raw.astype(jnp.float32) * dq_rows, axis=0), ("dp", "ctx"))
    return (grad_queries[None], grad_keys[None], grad_values[None], gain_total)


def solution(mesh):
    in_specs = (
        P("dp", "ctx", None),
        P("dp", "ctx", None),
        P("dp", "ctx", None),
        P("dp", "ctx", None),
        P("dp", None, "ctx"),
        P(),
        P(),
    )
    out_specs = (P("dp", "ctx", None), P("dp", "ctx", None), P("dp", "ctx", None), P())
    return jax.shard_map(body, mesh=mesh, in_specs=in_specs, out_specs=out_specs, check_vma=False)
```

profile of v0, /device:TPU:0, one launch (start us, length us, event | category | flops | bytes accessed | tf_op | source)
XLA Modules:
  0.0 272.5 jit_solution(3529592541120777040)
XLA Ops:
  0.7 0.9 reshape_squeeze.12
  1.7 1.7 clamp_reduce_fusion.3
  3.9 0.9 reshape_squeeze.15
  5.4 1.6 collective-permute-start
  9.4 1.6 collective-permute-start.3
  11.9 1.1 collective-permute-start.6
  19.4 0.9 fusion.193
  20.3 0.9 fusion.203
  26.8 1.0 copy.380
  28.0 0.9 reshape_reshape_transpose.2
  28.9 1.2 reshape.1667
  33.0 0.8 copy-done.5
  34.6 3.2 %collective-permute-start.2 = (bf16[2,256,256]{2,1,0:T(8,128)(2,1)S(1)}, bf16[2,256,256]{2,1,0:T(8,128)(2,1)S(1)}, u32[]{:S(2)}, u32[]{:S(2)}) collective-permute-start(bf16[2,256,256]{2,1,0:T(8,128)(2,1)S(1)} %maximum_select_fusion.7), channel_id=1, source_target_pairs={{0,2},{2,0},{1,3},{3,1},{4,6},{6,4},{5,7},{7,5},{8,10},{10,8},{9,1... | collective-permute-start | bytes 786440 | tf_op jit(solution)/shard_map/ppermute | solution.py:18
  37.9 0.8 copy.373
  39.3 0.8 maximum_select_fusion.9
  40.1 2.0 collective-permute-start.7
  42.1 0.8 maximum_select_fusion.8
  42.9 1.5 collective-permute-start.4
  44.5 1.0 collective-permute-done.2
  47.9 9.2 %collective-permute-done.4 = bf16[2,256,256]{2,1,0:T(8,128)(2,1)} collective-permute-done((bf16[2,256,256]{2,1,0:T(8,128)(2,1)}, bf16[2,256,256]{2,1,0:T(8,128)(2,1)}, u32[]{:S(2)}, u32[]{:S(2)}) %collective-permute-start.4) | collective-permute-done | bytes 262176 | tf_op jit(solution)/shard_map/ppermute | solution.py:18
  57.1 1.3 maximum_select_fusion.4
  58.4 2.4 collective-permute-start.5
  60.8 0.8 fusion.213
  62.4 0.8 fusion.49
  63.1 3.0 %collective-permute-start.11 = (bf16[2,256,256]{2,1,0:T(8,128)(2,1)}, bf16[2,256,256]{2,1,0:T(8,128)(2,1)}, u32[]{:S(2)}, u32[]{:S(2)}) collective-permute-start(bf16[2,256,256]{2,1,0:T(8,128)(2,1)} %fusion.49), channel_id=1, source_target_pairs={{0,2},{2,0},{1,3},{3,1},{4,6},{6,4},{5,7},{7,5},{8,10},{10,8},{9,1... | collective-permute-start | bytes 786440 | tf_op jit(solution)/shard_map/ppermute | solution.py:18
  66.1 2.2 maximum_select_fusion.5
  68.4 4.8 %collective-permute-done.5 = bf16[2,512,256]{2,1,0:T(8,128)(2,1)} collective-permute-done((bf16[2,512,256]{2,1,0:T(8,128)(2,1)S(1)}, bf16[2,512,256]{2,1,0:T(8,128)(2,1)}, u32[]{:S(2)}, u32[]{:S(2)}) %collective-permute-start.5) | collective-permute-done | bytes 524320 | tf_op jit(solution)/shard_map/ppermute | solution.py:18
  73.2 1.4 maximum_select_fusion.1
  77.0 1.5 pad_maximum_fusion.1
  78.5 3.0 %reshape.1673 = f32[2,2,512,256]{2,1,3,0:T(2,128)S(1)} reshape(f32[2,1024,256]{1,2,0:T(8,128)} %pad_maximum_fusion.1) | data formatting | bytes 4194304 | tf_op jit(solution)/shard_map/reshape | solution.py:137
  81.6 2.9 %fusion.212 = (f32[2,1,512,256]{2,1,3,0:T(1,128)}, f32[2,1,512,256]{2,1,3,0:T(1,128)}) fusion(f32[2,2,512,256]{2,1,3,0:T(2,128)S(1)} %reshape.1673), kind=kLoop, calls=%fused_computation.413 | loop fusion | bytes 4194304 | tf_op jit(solution)/shard_map/slice | solution.py:139
  84.5 2.3 copy.151
  86.9 2.4 copy.152
  89.4 2.7 collective-permute-start.13
  92.1 1.8 maximum_select_fusion.2
  93.8 3.7 %collective-permute-start.9 = (bf16[2,1024,256]{2,1,0:T(8,128)(2,1)S(1)}, bf16[2,1024,256]{2,1,0:T(8,128)(2,1)S(1)}, u32[]{:S(2)}, u32[]{:S(2)}) collective-permute-start(bf16[2,1024,256]{2,1,0:T(8,128)(2,1)S(1)} %maximum_select_fusion.2), channel_id=1, source_target_pairs={{0,8},{8,0},{1,9},{9,1},{2,10},{10,2},{3,11},{11,3},{4,12},{12,4},... | collective-permute-start | bytes 3145736 | tf_op jit(solution)/shard_map/ppermute | solution.py:18
  97.5 1.0 fusion.58
  98.5 0.9 copy.191
  99.4 1.0 bitcast_add_fusion.5
  100.4 0.7 fusion.68
  101.1 1.7 collective-permute-start.12
  102.8 2.1 collective-permute-done.13
  105.2 18.4 %collective-permute-done.9 = bf16[2,1024,256]{2,1,0:T(8,128)(2,1)S(1)} collective-permute-done((bf16[2,1024,256]{2,1,0:T(8,128)(2,1)S(1)}, bf16[2,1024,256]{2,1,0:T(8,128)(2,1)S(1)}, u32[]{:S(2)}, u32[]{:S(2)}) %collective-permute-start.9) | collective-permute-done | bytes 1048608 | tf_op jit(solution)/shard_map/ppermute | solution.py:18
  127.4 2.5 pad_maximum_fusion
  129.9 6.6 %reshape.1677 = f32[2,2,1024,256]{2,1,3,0:T(2,128)} reshape(f32[2,2048,256]{1,2,0:T(8,128)} %pad_maximum_fusion) | data formatting | bytes 8388608 | tf_op jit(solution)/shard_map/reshape | solution.py:137
  136.5 9.1 %fusion.211 = (f32[2,1,1024,256]{2,1,3,0:T(1,128)}, f32[2,1,1024,256]{2,1,3,0:T(1,128)}) fusion(f32[2,2,1024,256]{2,1,3,0:T(2,128)} %reshape.1677), kind=kLoop, calls=%fused_computation.412 | loop fusion | bytes 8388608 | tf_op jit(solution)/shard_map/slice | solution.py:139
  145.6 4.6 %copy.157 = f32[2,1,1024,256]{3,2,0,1:T(8,128)S(1)} copy(f32[2,1,1024,256]{2,1,3,0:T(1,128)} %get-tuple-element.141) | data formatting | bytes 4194304
  150.2 6.0 %copy.158 = f32[2,1,1024,256]{3,2,0,1:T(8,128)} copy(f32[2,1,1024,256]{2,1,3,0:T(1,128)} %get-tuple-element.142) | data formatting | bytes 4194304
  156.2 1.9 fusion.36
  158.3 3.1 %collective-permute-start.14 = (bf16[2,256,256]{2,1,0:T(8,128)(2,1)S(1)}, bf16[2,256,256]{2,1,0:T(8,128)(2,1)S(1)}, u32[]{:S(2)}, u32[]{:S(2)}) collective-permute-start(bf16[2,256,256]{2,1,0:T(8,128)(2,1)S(1)} %fusion.50), channel_id=1, source_target_pairs={{0,2},{2,0},{1,3},{3,1},{4,6},{6,4},{5,7},{7,5},{8,10},{10,8},{9,1... | collective-permute-start | bytes 786440 | tf_op jit(solution)/shard_map/ppermute | solution.py:18
  161.7 1.1 fusion.55
  162.8 0.9 copy.192
  163.7 3.3 %collective-permute-done.14 = bf16[2,256,256]{2,1,0:T(8,128)(2,1)S(1)} collective-permute-done((bf16[2,256,256]{2,1,0:T(8,128)(2,1)S(1)}, bf16[2,256,256]{2,1,0:T(8,128)(2,1)S(1)}, u32[]{:S(2)}, u32[]{:S(2)}) %collective-permute-start.14) | collective-permute-done | bytes 262176 | tf_op jit(solution)/shard_map/ppermute | solution.py:18
  167.1 0.8 collective-permute-start.15
  167.9 14.9 %collective-permute-done.16 = bf16[2,1024,256]{2,1,0:T(8,128)(2,1)S(1)} collective-permute-done((bf16[2,1024,256]{2,1,0:T(8,128)(2,1)S(1)}, bf16[2,1024,256]{2,1,0:T(8,128)(2,1)S(1)}, u32[]{:S(2)}, u32[]{:S(2)}) %collective-permute-start.16) | collective-permute-done | bytes 1048608 | tf_op jit(solution)/shard_map/ppermute | solution.py:18
  185.6 6.9 %collective-permute-done.17 = bf16[2,512,256]{2,1,0:T(8,128)(2,1)S(1)} collective-permute-done((bf16[2,512,256]{2,1,0:T(8,128)(2,1)S(1)}, bf16[2,512,256]{2,1,0:T(8,128)(2,1)S(1)}, u32[]{:S(2)}, u32[]{:S(2)}) %collective-permute-start.17) | collective-permute-done | bytes 524320 | tf_op jit(solution)/shard_map/ppermute | solution.py:18
  193.5 3.5 %collective-permute-start.18 = (bf16[2,256,256]{2,1,0:T(8,128)(2,1)}, bf16[2,256,256]{2,1,0:T(8,128)(2,1)S(1)}, u32[]{:S(2)}, u32[]{:S(2)}) collective-permute-start(bf16[2,256,256]{2,1,0:T(8,128)(2,1)} %fusion.51), channel_id=1, source_target_pairs={{0,2},{2,0},{1,3},{3,1},{4,6},{6,4},{5,7},{7,5},{8,10},{10,8},{9,1... | collective-permute-start | bytes 786440 | tf_op jit(solution)/shard_map/ppermute | solution.py:18
  197.1 1.2 fusion.6
  199.1 63.0 %psum.7 = f32[256]{0:T(256)} all-reduce(f32[256]{0:T(256)S(1)} %bitcast.569), channel_id=1, replica_groups=mesh['dp'=8,'ctx'=16] {'dp','ctx'}, use_global_device_ids=true, to_apply=%region_1.2 | all-reduce | flops 256 | bytes 2048 | tf_op jit(solution)/shard_map/psum | solution.py:217
  262.3 1.5 collective-permute-start.19
  264.4 3.2 %collective-permute-done.19 = bf16[2,128,256]{2,1,0:T(8,128)(2,1)S(1)} collective-permute-done((bf16[2,128,256]{2,1,0:T(8,128)(2,1)S(1)}, bf16[2,128,256]{2,1,0:T(8,128)(2,1)S(1)}, u32[]{:S(2)}, u32[]{:S(2)}) %collective-permute-start.19) | collective-permute-done | bytes 131104 | tf_op jit(solution)/shard_map/ppermute | solution.py:18
  267.9 2.4 fusion.3
  270.7 0.7 convert_element_type.423
  271.5 0.7 convert_element_type.420
  (296 shorter events, 36.4 us)
Async XLA Ops:
  3.4 5.4 %copy-start.28 = (s32[2]{0:T(128)}, s32[2]{0:T(128)S(1)}, u32[]{:S(2)}) copy-start(s32[2]{0:T(128)S(1)} %get-tuple-element.178) | copy-start | bytes 28
  3.4 5.4 %copy-start.30 = (s32[2]{0:T(128)}, s32[2]{0:T(128)S(1)}, u32[]{:S(2)}) copy-start(s32[2]{0:T(128)S(1)} %get-tuple-element.181) | copy-start | bytes 28
  3.4 5.4 %copy-start.32 = (s32[2]{0:T(128)}, s32[2]{0:T(128)S(1)}, u32[]{:S(2)}) copy-start(s32[2]{0:T(128)S(1)} %get-tuple-element.118) | copy-start | bytes 28
  3.4 5.4 %copy-start.34 = (s32[2]{0:T(128)}, s32[2]{0:T(128)S(1)}, u32[]{:S(2)}) copy-start(s32[2]{0:T(128)S(1)} %get-tuple-element.164) | copy-start | bytes 28
  5.4 26.5 %collective-permute-start = (bf16[2,128,256]{2,1,0:T(8,128)(2,1)S(1)}, bf16[2,128,256]{2,1,0:T(8,128)(2,1)S(1)}, u32[]{:S(2)}, u32[]{:S(2)}) collective-permute-start(bf16[2,128,256]{2,1,0:T(8,128)(2,1)S(1)} %bitcast_dynamic-update-slice_fusion.6), channel_id=1, source_target_pairs={{0,1},{1,0},{2,3},{3,2},{4,5},{5,4},{6,7},{7,6},{8,9},{9,8},{10,11... | collective-permute-start | bytes 393224 | tf_op jit(solution)/shard_map/ppermute | solution.py:18
  7.6 5.4 %copy-start.46 = (f32[1,2,256]{2,1,0:T(2,128)S(1)}, f32[1,2,256]{2,1,0:T(2,128)}, u32[]{:S(2)}) copy-start(f32[1,2,256]{2,1,0:T(2,128)} %param.11) | copy-start | bytes 6148
  7.9 26.5 %collective-permute-start.1 = (bf16[2,128,256]{2,1,0:T(8,128)(2,1)S(1)}, bf16[2,128,256]{2,1,0:T(8,128)(2,1)S(1)}, u32[]{:S(2)}, u32[]{:S(2)}) collective-permute-start(bf16[2,128,256]{2,1,0:T(8,128)(2,1)S(1)} %bitcast_dynamic-update-slice_fusion.4), channel_id=1, source_target_pairs={{0,1},{1,0},{2,3},{3,2},{4,5},{5,4},{6,7},{7,6},{8,9},{9,8},{10,11... | collective-permute-start | bytes 393224 | tf_op jit(solution)/shard_map/ppermute | solution.py:18
  8.5 8.3 %copy-start.25 = (bf16[1,256,256]{2,1,0:T(8,128)(2,1)S(1)}, bf16[1,256,256]{2,1,0:T(8,128)(2,1)}, u32[]{:S(2)}) copy-start(bf16[1,256,256]{2,1,0:T(8,128)(2,1)} %param.10) | copy-start | bytes 393220
  9.4 32.7 %collective-permute-start.3 = (bf16[2,128,256]{2,1,0:T(8,128)(2,1)S(1)}, bf16[2,128,256]{2,1,0:T(8,128)(2,1)S(1)}, u32[]{:S(2)}, u32[]{:S(2)}) collective-permute-start(bf16[2,128,256]{2,1,0:T(8,128)(2,1)S(1)} %bitcast_dynamic-update-slice_fusion.2), channel_id=1, source_target_pairs={{0,1},{1,0},{2,3},{3,2},{4,5},{5,4},{6,7},{7,6},{8,9},{9,8},{10,11... | collective-permute-start | bytes 393224 | tf_op jit(solution)/shard_map/ppermute | solution.py:18
  11.9 27.4 %collective-permute-start.6 = (bf16[2,128,256]{2,1,0:T(8,128)(2,1)S(1)}, bf16[2,128,256]{2,1,0:T(8,128)(2,1)S(1)}, u32[]{:S(2)}, u32[]{:S(2)}) collective-permute-start(bf16[2,128,256]{2,1,0:T(8,128)(2,1)S(1)} %bitcast_dynamic-update-slice_fusion), channel_id=1, source_target_pairs={{0,1},{1,0},{2,3},{3,2},{4,5},{5,4},{6,7},{7,6},{8,9},{9,8},{10,11... | collective-permute-start | bytes 393224 | tf_op jit(solution)/shard_map/ppermute | solution.py:18
  13.0 8.2 %copy-start.57 = (s32[2,2]{1,0:T(2,128)}, s32[2,2]{1,0:T(2,128)S(1)}, u32[]{:S(2)}) copy-start(s32[2,2]{1,0:T(2,128)S(1)} %iota_clamp_fusion) | copy-start | bytes 52
  13.0 8.6 %copy-start.51 = (f32[2,2]{1,0:T(2,128)}, f32[2,2]{1,0:T(2,128)S(1)}, u32[]{:S(2)}) copy-start(f32[2,2]{1,0:T(2,128)S(1)} %and_convert_fusion.8) | copy-start | bytes 52
  24.8 5.3 %copy-start.42 = (s32[2,1]{1,0:T(2,128)S(1)}, s32[2,1]{1,0:T(2,128)}, u32[]{:S(2)}) copy-start(s32[2,1]{1,0:T(2,128)} %get-tuple-element.179) | copy-start | bytes 28
  24.8 5.3 %copy-start.43 = (s32[2,1]{1,0:T(2,128)S(1)}, s32[2,1]{1,0:T(2,128)}, u32[]{:S(2)}) copy-start(s32[2,1]{1,0:T(2,128)} %get-tuple-element.180) | copy-start | bytes 28
  24.9 5.5 %copy-start.40 = (s32[2,1]{1,0:T(2,128)S(1)}, s32[2,1]{1,0:T(2,128)}, u32[]{:S(2)}) copy-start(s32[2,1]{1,0:T(2,128)} %get-tuple-element.176) | copy-start | bytes 28
  24.9 5.5 %copy-start.41 = (s32[2,1]{1,0:T(2,128)S(1)}, s32[2,1]{1,0:T(2,128)}, u32[]{:S(2)}) copy-start(s32[2,1]{1,0:T(2,128)} %get-tuple-element.177) | copy-start | bytes 28
  24.9 5.6 %copy-start.38 = (s32[2,1]{1,0:T(2,128)S(1)}, s32[2,1]{1,0:T(2,128)}, u32[]{:S(2)}) copy-start(s32[2,1]{1,0:T(2,128)} %get-tuple-element.119) | copy-start | bytes 28
  24.9 5.6 %copy-start.39 = (s32[2,1]{1,0:T(2,128)S(1)}, s32[2,1]{1,0:T(2,128)}, u32[]{:S(2)}) copy-start(s32[2,1]{1,0:T(2,128)} %get-tuple-element.120) | copy-start | bytes 28
  24.9 5.7 %copy-start.33 = (s32[2]{0:T(128)S(1)}, s32[2]{0:T(128)}, u32[]{:S(2)}) copy-start(s32[2]{0:T(128)} %copy-done.32) | copy-start | bytes 28
  24.9 5.7 %copy-start.35 = (s32[2]{0:T(128)S(1)}, s32[2]{0:T(128)}, u32[]{:S(2)}) copy-start(s32[2]{0:T(128)} %copy-done.34) | copy-start | bytes 28
  24.9 6.3 %copy-start.29 = (s32[2]{0:T(128)S(1)}, s32[2]{0:T(128)}, u32[]{:S(2)}) copy-start(s32[2]{0:T(128)} %copy-done.28) | copy-start | bytes 28
  24.9 6.3 %copy-start.31 = (s32[2]{0:T(128)S(1)}, s32[2]{0:T(128)}, u32[]{:S(2)}) copy-start(s32[2]{0:T(128)} %copy-done.30) | copy-start | bytes 28
  25.3 6.7 %copy-start.62 = (f32[2,1,128]{2,1,0:T(1,128)S(1)}, f32[2,1,128]{2,1,0:T(1,128)}, u32[]{:S(2)}) copy-start(f32[2,1,128]{2,1,0:T(1,128)} %fusion.197) | copy-start | bytes 3076
  33.0 12.7 %copy-start.61 = (f32[2,1,128]{2,1,0:T(1,128)S(1)}, f32[2,1,128]{2,1,0:T(1,128)}, u32[]{:S(2)}) copy-start(f32[2,1,128]{2,1,0:T(1,128)} %fusion.187) | copy-start | bytes 3076
  34.6 10.8 %collective-permute-start.2 = (bf16[2,256,256]{2,1,0:T(8,128)(2,1)S(1)}, bf16[2,256,256]{2,1,0:T(8,128)(2,1)S(1)}, u32[]{:S(2)}, u32[]{:S(2)}) collective-permute-start(bf16[2,256,256]{2,1,0:T(8,128)(2,1)S(1)} %maximum_select_fusion.7), channel_id=1, source_target_pairs={{0,2},{2,0},{1,3},{3,1},{4,6},{6,4},{5,7},{7,5},{8,10},{10,8},{9,1... | collective-permute-start | bytes 786440 | tf_op jit(solution)/shard_map/ppermute | solution.py:18
  38.7 58.8 %collective-permute-start.10 = (bf16[2,128,256]{2,1,0:T(8,128)(2,1)}, bf16[2,128,256]{2,1,0:T(8,128)(2,1)}, u32[]{:S(2)}, u32[]{:S(2)}) collective-permute-start(bf16[2,128,256]{2,1,0:T(8,128)(2,1)} %fusion.67), channel_id=1, source_target_pairs={{0,1},{1,0},{2,3},{3,2},{4,5},{5,4},{6,7},{7,6},{8,9},{9,8},{10,11... | collective-permute-start | bytes 393224 | tf_op jit(solution)/shard_map/ppermute | solution.py:18
  40.1 26.1 %collective-permute-start.7 = (bf16[2,256,256]{2,1,0:T(8,128)(2,1)}, bf16[2,256,256]{2,1,0:T(8,128)(2,1)}, u32[]{:S(2)}, u32[]{:S(2)}) collective-permute-start(bf16[2,256,256]{2,1,0:T(8,128)(2,1)} %maximum_select_fusion.9), channel_id=1, source_target_pairs={{0,2},{2,0},{1,3},{3,1},{4,6},{6,4},{5,7},{7,5},{8,10},{10,8},{9,1... | collective-permute-start | bytes 786440 | tf_op jit(solution)/shard_map/ppermute | solution.py:18
  42.9 14.2 %collective-permute-start.4 = (bf16[2,256,256]{2,1,0:T(8,128)(2,1)}, bf16[2,256,256]{2,1,0:T(8,128)(2,1)}, u32[]{:S(2)}, u32[]{:S(2)}) collective-permute-start(bf16[2,256,256]{2,1,0:T(8,128)(2,1)} %maximum_select_fusion.8), channel_id=1, source_target_pairs={{0,2},{2,0},{1,3},{3,1},{4,6},{6,4},{5,7},{7,5},{8,10},{10,8},{9,1... | collective-permute-start | bytes 786440 | tf_op jit(solution)/shard_map/ppermute | solution.py:18
  58.4 14.8 %collective-permute-start.5 = (bf16[2,512,256]{2,1,0:T(8,128)(2,1)S(1)}, bf16[2,512,256]{2,1,0:T(8,128)(2,1)}, u32[]{:S(2)}, u32[]{:S(2)}) collective-permute-start(bf16[2,512,256]{2,1,0:T(8,128)(2,1)S(1)} %maximum_select_fusion.4), channel_id=1, source_target_pairs={{0,4},{4,0},{1,5},{5,1},{2,6},{6,2},{3,7},{7,3},{8,12},{12,8},{9,1... | collective-permute-start | bytes 1572872 | tf_op jit(solution)/shard_map/ppermute | solution.py:18
  62.3 12.3 %copy-start.19 = (bf16[2,1,16384]{2,0,1:T(2,128)(2,1)S(1)}, bf16[2,1,16384]{2,0,1:T(2,128)(2,1)}, u32[]{:S(2)}) copy-start(bf16[2,1,16384]{2,0,1:T(2,128)(2,1)} %copy.384) | copy-start | bytes 196612
  62.3 12.3 %copy-start.27 = (f32[1,2,8,128]{3,1,2,0:T(2,128)S(1)}, f32[1,2,8,128]{3,1,2,0:T(2,128)}, u32[]{:S(2)}) copy-start(f32[1,2,8,128]{3,1,2,0:T(2,128)} %copy.393) | copy-start | bytes 24580
  62.3 12.3 %copy-start.50 = (f32[2]{0:T(128)S(1)}, f32[2]{0:T(128)}, u32[]{:S(2)}) copy-start(f32[2]{0:T(128)} %copy-done.49) | copy-start | bytes 28
  62.4 12.3 %copy-start.60 = (f32[2,1,128]{2,1,0:T(1,128)S(1)}, f32[2,1,128]{2,1,0:T(1,128)}, u32[]{:S(2)}) copy-start(f32[2,1,128]{2,1,0:T(1,128)} %fusion.177) | copy-start | bytes 3076
  63.1 36.2 %collective-permute-start.11 = (bf16[2,256,256]{2,1,0:T(8,128)(2,1)}, bf16[2,256,256]{2,1,0:T(8,128)(2,1)}, u32[]{:S(2)}, u32[]{:S(2)}) collective-permute-start(bf16[2,256,256]{2,1,0:T(8,128)(2,1)} %fusion.49), channel_id=1, source_target_pairs={{0,2},{2,0},{1,3},{3,1},{4,6},{6,4},{5,7},{7,5},{8,10},{10,8},{9,1... | collective-permute-start | bytes 786440 | tf_op jit(solution)/shard_map/ppermute | solution.py:18
  68.3 23.8 %collective-permute-start.8 = (bf16[2,512,256]{2,1,0:T(8,128)(2,1)}, bf16[2,512,256]{2,1,0:T(8,128)(2,1)}, u32[]{:S(2)}, u32[]{:S(2)}) collective-permute-start(bf16[2,512,256]{2,1,0:T(8,128)(2,1)} %maximum_select_fusion.5), channel_id=1, source_target_pairs={{0,4},{4,0},{1,5},{5,1},{2,6},{6,2},{3,7},{7,3},{8,12},{12,8},{9,1... | collective-permute-start | bytes 1572872 | tf_op jit(solution)/shard_map/ppermute | solution.py:18
  89.2 8.3 %copy-start.6 = (f32[2,256,256]{2,1,0:T(8,128)S(1)}, f32[2,256,256]{2,1,0:T(8,128)}, u32[]{:S(2)}) copy-start(f32[2,256,256]{2,1,0:T(8,128)} %copy-done.5) | copy-start | bytes 1572868
  89.4 15.5 %collective-permute-start.13 = (bf16[2,512,256]{2,1,0:T(8,128)(2,1)S(1)}, bf16[2,512,256]{2,1,0:T(8,128)(2,1)S(1)}, u32[]{:S(2)}, u32[]{:S(2)}) collective-permute-start(bf16[2,512,256]{2,1,0:T(8,128)(2,1)S(1)} %fusion.42), channel_id=1, source_target_pairs={{0,4},{4,0},{1,5},{5,1},{2,6},{6,2},{3,7},{7,3},{8,12},{12,8},{9,1... | collective-permute-start | bytes 1572872 | tf_op jit(solution)/shard_map/ppermute | solution.py:18
  93.8 29.7 %collective-permute-start.9 = (bf16[2,1024,256]{2,1,0:T(8,128)(2,1)S(1)}, bf16[2,1024,256]{2,1,0:T(8,128)(2,1)S(1)}, u32[]{:S(2)}, u32[]{:S(2)}) collective-permute-start(bf16[2,1024,256]{2,1,0:T(8,128)(2,1)S(1)} %maximum_select_fusion.2), channel_id=1, source_target_pairs={{0,8},{8,0},{1,9},{9,1},{2,10},{10,2},{3,11},{11,3},{4,12},{12,4},... | collective-permute-start | bytes 3145736 | tf_op jit(solution)/shard_map/ppermute | solution.py:18
  101.1 60.6 %collective-permute-start.12 = (bf16[2,128,256]{2,1,0:T(8,128)(2,1)}, bf16[2,128,256]{2,1,0:T(8,128)(2,1)}, u32[]{:S(2)}, u32[]{:S(2)}) collective-permute-start(bf16[2,128,256]{2,1,0:T(8,128)(2,1)} %fusion.68), channel_id=1, source_target_pairs={{0,1},{1,0},{2,3},{3,2},{4,5},{5,4},{6,7},{7,6},{8,9},{9,8},{10,11... | collective-permute-start | bytes 393224 | tf_op jit(solution)/shard_map/ppermute | solution.py:18
  105.1 19.0 %copy-start.18 = (bf16[2,1,16384]{2,0,1:T(2,128)(2,1)S(1)}, bf16[2,1,16384]{2,0,1:T(2,128)(2,1)}, u32[]{:S(2)}) copy-start(bf16[2,1,16384]{2,0,1:T(2,128)(2,1)} %copy.388) | copy-start | bytes 196612
  105.1 19.0 %copy-start.48 = (f32[2]{0:T(128)S(1)}, f32[2]{0:T(128)}, u32[]{:S(2)}) copy-start(f32[2]{0:T(128)} %copy-done.47) | copy-start | bytes 28
  105.2 19.0 %copy-start.59 = (f32[2,1,128]{2,1,0:T(1,128)S(1)}, f32[2,1,128]{2,1,0:T(1,128)}, u32[]{:S(2)}) copy-start(f32[2,1,128]{2,1,0:T(1,128)} %fusion.167) | copy-start | bytes 3076
  156.2 5.5 %copy-start.8 = (f32[2,256,256]{2,1,0:T(8,128)S(1)}, f32[2,256,256]{2,1,0:T(8,128)}, u32[]{:S(2)}) copy-start(f32[2,256,256]{2,1,0:T(8,128)} %copy-done.7) | copy-start | bytes 1572868
  158.1 24.7 %collective-permute-start.16 = (bf16[2,1024,256]{2,1,0:T(8,128)(2,1)S(1)}, bf16[2,1024,256]{2,1,0:T(8,128)(2,1)S(1)}, u32[]{:S(2)}, u32[]{:S(2)}) collective-permute-start(bf16[2,1024,256]{2,1,0:T(8,128)(2,1)S(1)} %fusion.36), channel_id=1, source_target_pairs={{0,8},{8,0},{1,9},{9,1},{2,10},{10,2},{3,11},{11,3},{4,12},{12,4},... | collective-permute-start | bytes 3145736 | tf_op jit(solution)/shard_map/ppermute | solution.py:18
  158.3 8.7 %collective-permute-start.14 = (bf16[2,256,256]{2,1,0:T(8,128)(2,1)S(1)}, bf16[2,256,256]{2,1,0:T(8,128)(2,1)S(1)}, u32[]{:S(2)}, u32[]{:S(2)}) collective-permute-start(bf16[2,256,256]{2,1,0:T(8,128)(2,1)S(1)} %fusion.50), channel_id=1, source_target_pairs={{0,2},{2,0},{1,3},{3,1},{4,6},{6,4},{5,7},{7,5},{8,10},{10,8},{9,1... | collective-permute-start | bytes 786440 | tf_op jit(solution)/shard_map/ppermute | solution.py:18
  161.6 21.2 %copy-start = (f32[2,1,1024,256]{3,2,0,1:T(8,128)S(1)}, f32[2,1,1024,256]{3,2,0,1:T(8,128)}, u32[]{:S(2)}) copy-start(f32[2,1,1024,256]{3,2,0,1:T(8,128)} %copy.158) | copy-start | bytes 6291460
  167.1 16.3 %copy-start.12 = (bf16[2,1024,256]{2,1,0:T(8,128)(2,1)S(1)}, bf16[2,1024,256]{2,1,0:T(8,128)(2,1)}, u32[]{:S(2)}) copy-start(bf16[2,1024,256]{2,1,0:T(8,128)(2,1)} %copy-done.11) | copy-start | bytes 3145732
  167.1 16.3 %copy-start.16 = (bf16[2,128,1024]{2,1,0:T(8,128)(2,1)S(1)}, bf16[2,128,1024]{2,1,0:T(8,128)(2,1)}, u32[]{:S(2)}) copy-start(bf16[2,128,1024]{2,1,0:T(8,128)(2,1)} %copy-done.15) | copy-start | bytes 1572868
  167.1 16.7 %collective-permute-start.15 = (bf16[2,128,256]{2,1,0:T(8,128)(2,1)S(1)}, bf16[2,128,256]{2,1,0:T(8,128)(2,1)S(1)}, u32[]{:S(2)}, u32[]{:S(2)}) collective-permute-start(bf16[2,128,256]{2,1,0:T(8,128)(2,1)S(1)} %fusion.69), channel_id=1, source_target_pairs={{0,1},{1,0},{2,3},{3,2},{4,5},{5,4},{6,7},{7,6},{8,9},{9,8},{10,11... | collective-permute-start | bytes 393224 | tf_op jit(solution)/shard_map/ppermute | solution.py:18
  183.3 9.3 %collective-permute-start.17 = (bf16[2,512,256]{2,1,0:T(8,128)(2,1)S(1)}, bf16[2,512,256]{2,1,0:T(8,128)(2,1)S(1)}, u32[]{:S(2)}, u32[]{:S(2)}) collective-permute-start(bf16[2,512,256]{2,1,0:T(8,128)(2,1)S(1)} %fusion.43), channel_id=1, source_target_pairs={{0,4},{4,0},{1,5},{5,1},{2,6},{6,2},{3,7},{7,3},{8,12},{12,8},{9,1... | collective-permute-start | bytes 1572872 | tf_op jit(solution)/shard_map/ppermute | solution.py:18
  185.6 11.5 %copy-start.20 = (f32[2,2,16384]{2,1,0:T(2,128)S(1)}, f32[2,2,16384]{2,1,0:T(2,128)}, u32[]{:S(2)}) copy-start(f32[2,2,16384]{2,1,0:T(2,128)} %reshape_reshape_transpose.2) | copy-start | bytes 786436
  185.6 11.5 %copy-start.26 = (f32[1,2,128,128]{3,1,2,0:T(2,128)S(1)}, f32[1,2,128,128]{3,1,2,0:T(2,128)}, u32[]{:S(2)}) copy-start(f32[1,2,128,128]{3,1,2,0:T(2,128)} %copy.373) | copy-start | bytes 393220
  185.6 11.4 %copy-start.52 = (f32[2,2]{1,0:T(2,128)S(1)}, f32[2,2]{1,0:T(2,128)}, u32[]{:S(2)}) copy-start(f32[2,2]{1,0:T(2,128)} %copy-done.51) | copy-start | bytes 52
  185.6 11.4 %copy-start.53 = (f32[2,2]{1,0:T(2,128)S(1)}, f32[2,2]{1,0:T(2,128)}, u32[]{:S(2)}) copy-start(f32[2,2]{1,0:T(2,128)} %get-tuple-element.207) | copy-start | bytes 52
  185.6 11.4 %copy-start.54 = (f32[2,2]{1,0:T(2,128)S(1)}, f32[2,2]{1,0:T(2,128)}, u32[]{:S(2)}) copy-start(f32[2,2]{1,0:T(2,128)} %get-tuple-element.208) | copy-start | bytes 52
  185.6 11.4 %copy-start.55 = (f32[2,2]{1,0:T(2,128)S(1)}, f32[2,2]{1,0:T(2,128)}, u32[]{:S(2)}) copy-start(f32[2,2]{1,0:T(2,128)} %get-tuple-element.203) | copy-start | bytes 52
  185.6 11.4 %copy-start.56 = (f32[2,2]{1,0:T(2,128)S(1)}, f32[2,2]{1,0:T(2,128)}, u32[]{:S(2)}) copy-start(f32[2,2]{1,0:T(2,128)} %get-tuple-element.204) | copy-start | bytes 52
  185.6 11.4 %copy-start.58 = (s32[2,2]{1,0:T(2,128)S(1)}, s32[2,2]{1,0:T(2,128)}, u32[]{:S(2)}) copy-start(s32[2,2]{1,0:T(2,128)} %copy-done.57) | copy-start | bytes 52
  193.5 68.7 %collective-permute-start.18 = (bf16[2,256,256]{2,1,0:T(8,128)(2,1)}, bf16[2,256,256]{2,1,0:T(8,128)(2,1)S(1)}, u32[]{:S(2)}, u32[]{:S(2)}) collective-permute-start(bf16[2,256,256]{2,1,0:T(8,128)(2,1)} %fusion.51), channel_id=1, source_target_pairs={{0,2},{2,0},{1,3},{3,1},{4,6},{6,4},{5,7},{7,5},{8,10},{10,8},{9,1... | collective-permute-start | bytes 786440 | tf_op jit(solution)/shard_map/ppermute | solution.py:18
  198.3 65.4 %copy-start.37 = (f32[256]{0:T(256)S(1)}, f32[256]{0:T(256)}, u32[]{:S(2)}) copy-start(f32[256]{0:T(256)} %param.13) | copy-start | bytes 3076
  199.1 68.8 %copy-start.17 = (f32[2,2,32768]{2,1,0:T(2,128)S(1)}, f32[2,2,32768]{2,1,0:T(2,128)}, u32[]{:S(2)}) copy-start(f32[2,2,32768]{2,1,0:T(2,128)} %reshape.1667) | copy-start | bytes 1572868
  199.1 68.8 %copy-start.21 = (f32[1,2,128,256]{3,1,2,0:T(2,128)S(1)}, f32[1,2,128,256]{3,1,2,0:T(2,128)}, u32[]{:S(2)}) copy-start(f32[1,2,128,256]{3,1,2,0:T(2,128)} %copy.191) | copy-start | bytes 786436
  199.1 68.8 %copy-start.22 = (f32[1,2,128,256]{3,1,2,0:T(2,128)S(1)}, f32[1,2,128,256]{3,1,2,0:T(2,128)}, u32[]{:S(2)}) copy-start(f32[1,2,128,256]{3,1,2,0:T(2,128)} %copy.192) | copy-start | bytes 786436
  262.3 5.3 %collective-permute-start.19 = (bf16[2,128,256]{2,1,0:T(8,128)(2,1)S(1)}, bf16[2,128,256]{2,1,0:T(8,128)(2,1)S(1)}, u32[]{:S(2)}, u32[]{:S(2)}) collective-permute-start(bf16[2,128,256]{2,1,0:T(8,128)(2,1)S(1)} %fusion.70), channel_id=1, source_target_pairs={{0,1},{1,0},{2,3},{3,2},{4,5},{5,4},{6,7},{7,6},{8,9},{9,8},{10,11... | collective-permute-start | bytes 393224 | tf_op jit(solution)/shard_map/ppermute | solution.py:18
  (19 other events, 51.9 us)
where the time goes:
time: 277 us; the launch traced here: 273 us
  waiting for transfers between devices  63.6 us (23%)
  blocking collectives  63 us (23%)
  local copies, waits for them, and re-layouts  59.3 us (21%)
  starting transfers between devices  34.9 us (13%)
  other arithmetic  27.5 us (10%)
  matrix products  21.6 us (8%)
    ppermute x20, waiting for transfers between devices, swapped(): return lax.ppermute(block, axis, route)  63.6 us
    psum x1, blocking collectives, body(): lax.psum(jnp.sum(query_raw.astype(jnp.float32) * dq_rows, axis=0), ('dp',...  63 us
    ppermute x20, starting transfers between devices, swapped(): return lax.ppermute(block, axis, route)  34.9 us
    unnamed x153, local copies, waits for them, and re-layouts  24.8 us
    slice x3, local copies, waits for them, and re-layouts, swap_down(): kept_half = jnp.where(lower_half, halves[:, 0], halves[:, 1])  12.9 us
    reshape x3, local copies, waits for them, and re-layouts, swap_down(): halves = sums_kv.reshape(head_count, 2, -1, sums_kv.shape[-1])  10.3 us
    dot_general x25, matrix products, pick_blocks(): jnp.einsum('hsb,hbx->hsx', table, flat, precision=lax.Precision.HIGHEST,...  10.3 us
    select_n x10, other arithmetic, swap_up(): jnp.where(lower_half, jnp.concatenate([payload, partner], axis=1), jnp.co...  9.27 us
  transfers between devices with their start and end apart: 20, of which 9 were waited for; matrix products, arithmetic and copies ran while one was open for 34% of the time, Pallas kernels for 0%

commit v1 on v0

--- a/solution.py
+++ b/solution.py
@@ -214,7 +214,8 @@
     grad_queries = (dq_rows * q_gain).astype(jnp.bfloat16)
     grad_keys = to_rows(kv_acc[..., :head_dim]).astype(jnp.bfloat16)
     grad_values = to_rows(kv_acc[..., head_dim:]).astype(jnp.bfloat16)
-    gain_total = lax.psum(jnp.sum(query_raw.astype(jnp.float32) * dq_rows, axis=0), ("dp", "ctx"))
+    partial = lax.psum(jnp.sum(query_raw.astype(jnp.float32) * dq_rows, axis=0), "dp")
+    gain_total = lax.psum(partial, "ctx")
     return (grad_queries[None], grad_keys[None], grad_values[None], gain_total)
 
 

time: 277 us -> 263 us (0.949)
  blocking collectives: 63 us -> 49.3 us
    psum x1 -> x2, blocking collectives: 63 us -> 49.3 us  [the longest x1 36.7 us: body(): gain_total = lax.psum(partial, 'ctx')]
  transfers between devices with their start and end apart: 20 -> 20, of which waited for: 9 -> 9; matrix products, arithmetic and copies ran while one was open for 34% -> 36% of each run, Pallas kernels for 0% -> 0%
where the time goes in v1:
time: 263 us; the launch traced here: 259 us
  waiting for transfers between devices  63.2 us (24%)
  local copies, waits for them, and re-layouts  58.9 us (22%)
  blocking collectives  49.3 us (19%)
  starting transfers between devices  35.4 us (13%)
  other arithmetic  27.6 us (10%)
  matrix products  21.7 us (8%)
    ppermute x20, waiting for transfers between devices, swapped(): return lax.ppermute(block, axis, route)  63.2 us
    psum x1, blocking collectives, body(): gain_total = lax.psum(partial, 'ctx')  36.7 us
    ppermute x20, starting transfers between devices, swapped(): return lax.ppermute(block, axis, route)  35.4 us
    unnamed x153, local copies, waits for them, and re-layouts  24.5 us
    slice x3, local copies, waits for them, and re-layouts, swap_down(): kept_half = jnp.where(lower_half, halves[:, 0], halves[:, 1])  12.9 us
    psum x1, blocking collectives, body(): lax.psum(jnp.sum(query_raw.astype(jnp.float32) * dq_rows, axis=0), 'dp')  12.6 us
    dot_general x25, matrix products, pick_blocks(): jnp.einsum('hsb,hbx->hsx', table, flat, precision=lax.Precision.HIGHEST,...  10.3 us
    reshape x3, local copies, waits for them, and re-layouts, swap_down(): halves = sums_kv.reshape(head_count, 2, -1, sums_kv.shape[-1])  10.3 us
  transfers between devices with their start and end apart: 20, of which 9 were waited for; matrix products, arithmetic and copies ran while one was open for 36% of the time, Pallas kernels for 0%

profile of v1, /device:TPU:0, one launch (start us, length us, event | category | flops | bytes accessed | tf_op | source)
XLA Modules:
  0.0 258.7 jit_solution(1549517799884695533)
XLA Ops:
  0.7 0.9 reshape_squeeze.12
  1.7 1.7 clamp_reduce_fusion.3
  4.0 0.9 reshape_squeeze.15
  5.4 1.7 collective-permute-start
  9.4 1.7 collective-permute-start.3
  11.9 1.1 collective-permute-start.6
  19.4 0.9 fusion.193
  20.4 0.9 fusion.203
  26.9 1.0 copy.380
  28.1 0.9 reshape_reshape_transpose.2
  29.0 1.2 reshape.1667
  33.1 0.8 copy-done.5
  34.7 3.2 %collective-permute-start.2 = (bf16[2,256,256]{2,1,0:T(8,128)(2,1)S(1)}, bf16[2,256,256]{2,1,0:T(8,128)(2,1)S(1)}, u32[]{:S(2)}, u32[]{:S(2)}) collective-permute-start(bf16[2,256,256]{2,1,0:T(8,128)(2,1)S(1)} %maximum_select_fusion.7), channel_id=1, source_target_pairs={{0,2},{2,0},{1,3},{3,1},{4,6},{6,4},{5,7},{7,5},{8,10},{10,8},{9,1... | collective-permute-start | bytes 786440 | tf_op jit(solution)/shard_map/ppermute | solution.py:18
  38.1 0.8 copy.373
  39.5 0.8 maximum_select_fusion.9
  40.3 2.0 collective-permute-start.7
  42.3 0.8 maximum_select_fusion.8
  43.1 1.5 collective-permute-start.4
  44.6 1.0 collective-permute-done.2
  48.1 9.2 %collective-permute-done.4 = bf16[2,256,256]{2,1,0:T(8,128)(2,1)} collective-permute-done((bf16[2,256,256]{2,1,0:T(8,128)(2,1)}, bf16[2,256,256]{2,1,0:T(8,128)(2,1)}, u32[]{:S(2)}, u32[]{:S(2)}) %collective-permute-start.4) | collective-permute-done | bytes 262176 | tf_op jit(solution)/shard_map/ppermute | solution.py:18
  57.3 1.3 maximum_select_fusion.4
  58.6 2.4 collective-permute-start.5
  61.0 0.8 fusion.213
  62.5 0.8 fusion.49
  63.3 3.0 %collective-permute-start.11 = (bf16[2,256,256]{2,1,0:T(8,128)(2,1)}, bf16[2,256,256]{2,1,0:T(8,128)(2,1)}, u32[]{:S(2)}, u32[]{:S(2)}) collective-permute-start(bf16[2,256,256]{2,1,0:T(8,128)(2,1)} %fusion.49), channel_id=1, source_target_pairs={{0,2},{2,0},{1,3},{3,1},{4,6},{6,4},{5,7},{7,5},{8,10},{10,8},{9,1... | collective-permute-start | bytes 786440 | tf_op jit(solution)/shard_map/ppermute | solution.py:18
  66.3 2.1 maximum_select_fusion.5
  68.6 4.8 %collective-permute-done.5 = bf16[2,512,256]{2,1,0:T(8,128)(2,1)} collective-permute-done((bf16[2,512,256]{2,1,0:T(8,128)(2,1)S(1)}, bf16[2,512,256]{2,1,0:T(8,128)(2,1)}, u32[]{:S(2)}, u32[]{:S(2)}) %collective-permute-start.5) | collective-permute-done | bytes 524320 | tf_op jit(solution)/shard_map/ppermute | solution.py:18
  73.3 1.4 maximum_select_fusion.1
  77.2 1.5 pad_maximum_fusion.1
  78.7 3.0 %reshape.1673 = f32[2,2,512,256]{2,1,3,0:T(2,128)S(1)} reshape(f32[2,1024,256]{1,2,0:T(8,128)} %pad_maximum_fusion.1) | data formatting | bytes 4194304 | tf_op jit(solution)/shard_map/reshape | solution.py:137
  81.7 3.0 %fusion.212 = (f32[2,1,512,256]{2,1,3,0:T(1,128)}, f32[2,1,512,256]{2,1,3,0:T(1,128)}) fusion(f32[2,2,512,256]{2,1,3,0:T(2,128)S(1)} %reshape.1673), kind=kLoop, calls=%fused_computation.413 | loop fusion | bytes 4194304 | tf_op jit(solution)/shard_map/slice | solution.py:139
  84.7 2.3 copy.151
  87.1 2.4 copy.152
  89.6 2.7 %collective-permute-start.13 = (bf16[2,512,256]{2,1,0:T(8,128)(2,1)S(1)}, bf16[2,512,256]{2,1,0:T(8,128)(2,1)S(1)}, u32[]{:S(2)}, u32[]{:S(2)}) collective-permute-start(bf16[2,512,256]{2,1,0:T(8,128)(2,1)S(1)} %fusion.42), channel_id=1, source_target_pairs={{0,4},{4,0},{1,5},{5,1},{2,6},{6,2},{3,7},{7,3},{8,12},{12,8},{9,1... | collective-permute-start | bytes 1572872 | tf_op jit(solution)/shard_map/ppermute | solution.py:18
  92.3 1.8 maximum_select_fusion.2
  94.0 3.7 %collective-permute-start.9 = (bf16[2,1024,256]{2,1,0:T(8,128)(2,1)S(1)}, bf16[2,1024,256]{2,1,0:T(8,128)(2,1)S(1)}, u32[]{:S(2)}, u32[]{:S(2)}) collective-permute-start(bf16[2,1024,256]{2,1,0:T(8,128)(2,1)S(1)} %maximum_select_fusion.2), channel_id=1, source_target_pairs={{0,8},{8,0},{1,9},{9,1},{2,10},{10,2},{3,11},{11,3},{4,12},{12,4},... | collective-permute-start | bytes 3145736 | tf_op jit(solution)/shard_map/ppermute | solution.py:18
  97.7 1.0 fusion.58
  98.7 0.9 copy.191
  99.6 1.0 bitcast_add_fusion.5
  100.6 0.8 fusion.68
  101.4 1.7 collective-permute-start.12
  103.1 2.0 collective-permute-done.13
  105.4 18.4 %collective-permute-done.9 = bf16[2,1024,256]{2,1,0:T(8,128)(2,1)S(1)} collective-permute-done((bf16[2,1024,256]{2,1,0:T(8,128)(2,1)S(1)}, bf16[2,1024,256]{2,1,0:T(8,128)(2,1)S(1)}, u32[]{:S(2)}, u32[]{:S(2)}) %collective-permute-start.9) | collective-permute-done | bytes 1048608 | tf_op jit(solution)/shard_map/ppermute | solution.py:18
  127.6 2.5 pad_maximum_fusion
  130.1 6.6 %reshape.1677 = f32[2,2,1024,256]{2,1,3,0:T(2,128)} reshape(f32[2,2048,256]{1,2,0:T(8,128)} %pad_maximum_fusion) | data formatting | bytes 8388608 | tf_op jit(solution)/shard_map/reshape | solution.py:137
  136.7 9.1 %fusion.211 = (f32[2,1,1024,256]{2,1,3,0:T(1,128)}, f32[2,1,1024,256]{2,1,3,0:T(1,128)}) fusion(f32[2,2,1024,256]{2,1,3,0:T(2,128)} %reshape.1677), kind=kLoop, calls=%fused_computation.412 | loop fusion | bytes 8388608 | tf_op jit(solution)/shard_map/slice | solution.py:139
  145.8 4.6 %copy.157 = f32[2,1,1024,256]{3,2,0,1:T(8,128)S(1)} copy(f32[2,1,1024,256]{2,1,3,0:T(1,128)} %get-tuple-element.141) | data formatting | bytes 4194304
  150.4 6.1 %copy.158 = f32[2,1,1024,256]{3,2,0,1:T(8,128)} copy(f32[2,1,1024,256]{2,1,3,0:T(1,128)} %get-tuple-element.142) | data formatting | bytes 4194304
  156.4 1.9 fusion.36
  158.5 3.1 %collective-permute-start.14 = (bf16[2,256,256]{2,1,0:T(8,128)(2,1)S(1)}, bf16[2,256,256]{2,1,0:T(8,128)(2,1)S(1)}, u32[]{:S(2)}, u32[]{:S(2)}) collective-permute-start(bf16[2,256,256]{2,1,0:T(8,128)(2,1)S(1)} %fusion.50), channel_id=1, source_target_pairs={{0,2},{2,0},{1,3},{3,1},{4,6},{6,4},{5,7},{7,5},{8,10},{10,8},{9,1... | collective-permute-start | bytes 786440 | tf_op jit(solution)/shard_map/ppermute | solution.py:18
  162.0 1.1 fusion.55
  163.0 0.9 copy.192
  164.0 3.3 %collective-permute-done.14 = bf16[2,256,256]{2,1,0:T(8,128)(2,1)S(1)} collective-permute-done((bf16[2,256,256]{2,1,0:T(8,128)(2,1)S(1)}, bf16[2,256,256]{2,1,0:T(8,128)(2,1)S(1)}, u32[]{:S(2)}, u32[]{:S(2)}) %collective-permute-start.14) | collective-permute-done | bytes 262176 | tf_op jit(solution)/shard_map/ppermute | solution.py:18
  167.4 0.8 collective-permute-start.15
  168.2 14.6 %collective-permute-done.16 = bf16[2,1024,256]{2,1,0:T(8,128)(2,1)S(1)} collective-permute-done((bf16[2,1024,256]{2,1,0:T(8,128)(2,1)S(1)}, bf16[2,1024,256]{2,1,0:T(8,128)(2,1)S(1)}, u32[]{:S(2)}, u32[]{:S(2)}) %collective-permute-start.16) | collective-permute-done | bytes 1048608 | tf_op jit(solution)/shard_map/ppermute | solution.py:18
  185.7 6.9 %collective-permute-done.17 = bf16[2,512,256]{2,1,0:T(8,128)(2,1)S(1)} collective-permute-done((bf16[2,512,256]{2,1,0:T(8,128)(2,1)S(1)}, bf16[2,512,256]{2,1,0:T(8,128)(2,1)S(1)}, u32[]{:S(2)}, u32[]{:S(2)}) %collective-permute-start.17) | collective-permute-done | bytes 524320 | tf_op jit(solution)/shard_map/ppermute | solution.py:18
  192.8 0.7 fusion.51
  193.5 3.8 %collective-permute-start.18 = (bf16[2,256,256]{2,1,0:T(8,128)(2,1)}, bf16[2,256,256]{2,1,0:T(8,128)(2,1)S(1)}, u32[]{:S(2)}, u32[]{:S(2)}) collective-permute-start(bf16[2,256,256]{2,1,0:T(8,128)(2,1)} %fusion.51), channel_id=1, source_target_pairs={{0,2},{2,0},{1,3},{3,1},{4,6},{6,4},{5,7},{7,5},{8,10},{10,8},{9,1... | collective-permute-start | bytes 786440 | tf_op jit(solution)/shard_map/ppermute | solution.py:18
  197.3 1.2 fusion.6
  199.4 12.6 %psum.14 = f32[256]{0:T(256)S(1)} all-reduce(f32[256]{0:T(256)S(1)} %bitcast.569), channel_id=1, replica_groups=mesh['dp'=8,'ctx'=16] {'dp'}, use_global_device_ids=true, to_apply=%region_1.2 | all-reduce | flops 256 | bytes 2048 | tf_op jit(solution)/shard_map/psum | solution.py:217
  211.9 36.7 %psum.15 = f32[256]{0:T(256)} all-reduce(f32[256]{0:T(256)S(1)} %psum.14), channel_id=1, replica_groups=mesh['dp'=8,'ctx'=16] {'ctx'}, use_global_device_ids=true, to_apply=%region_2.3 | all-reduce | flops 256 | bytes 2048 | tf_op jit(solution)/shard_map/psum | solution.py:218
  248.8 1.4 collective-permute-start.19
  250.8 3.0 %collective-permute-done.19 = bf16[2,128,256]{2,1,0:T(8,128)(2,1)S(1)} collective-permute-done((bf16[2,128,256]{2,1,0:T(8,128)(2,1)S(1)}, bf16[2,128,256]{2,1,0:T(8,128)(2,1)S(1)}, u32[]{:S(2)}, u32[]{:S(2)}) %collective-permute-start.19) | collective-permute-done | bytes 131104 | tf_op jit(solution)/shard_map/ppermute | solution.py:18
  254.1 2.4 fusion.3
  (297 shorter events, 37.3 us)
Async XLA Ops:
  3.4 5.4 %copy-start.28 = (s32[2]{0:T(128)}, s32[2]{0:T(128)S(1)}, u32[]{:S(2)}) copy-start(s32[2]{0:T(128)S(1)} %get-tuple-element.178) | copy-start | bytes 28
  3.4 5.4 %copy-start.30 = (s32[2]{0:T(128)}, s32[2]{0:T(128)S(1)}, u32[]{:S(2)}) copy-start(s32[2]{0:T(128)S(1)} %get-tuple-element.181) | copy-start | bytes 28
  3.4 5.4 %copy-start.32 = (s32[2]{0:T(128)}, s32[2]{0:T(128)S(1)}, u32[]{:S(2)}) copy-start(s32[2]{0:T(128)S(1)} %get-tuple-element.118) | copy-start | bytes 28
  3.4 5.4 %copy-start.34 = (s32[2]{0:T(128)}, s32[2]{0:T(128)S(1)}, u32[]{:S(2)}) copy-start(s32[2]{0:T(128)S(1)} %get-tuple-element.164) | copy-start | bytes 28
  5.4 26.6 %collective-permute-start = (bf16[2,128,256]{2,1,0:T(8,128)(2,1)S(1)}, bf16[2,128,256]{2,1,0:T(8,128)(2,1)S(1)}, u32[]{:S(2)}, u32[]{:S(2)}) collective-permute-start(bf16[2,128,256]{2,1,0:T(8,128)(2,1)S(1)} %bitcast_dynamic-update-slice_fusion.6), channel_id=1, source_target_pairs={{0,1},{1,0},{2,3},{3,2},{4,5},{5,4},{6,7},{7,6},{8,9},{9,8},{10,11... | collective-permute-start | bytes 393224 | tf_op jit(solution)/shard_map/ppermute | solution.py:18
  7.6 5.4 %copy-start.46 = (f32[1,2,256]{2,1,0:T(2,128)S(1)}, f32[1,2,256]{2,1,0:T(2,128)}, u32[]{:S(2)}) copy-start(f32[1,2,256]{2,1,0:T(2,128)} %param.11) | copy-start | bytes 6148
  7.9 26.7 %collective-permute-start.1 = (bf16[2,128,256]{2,1,0:T(8,128)(2,1)S(1)}, bf16[2,128,256]{2,1,0:T(8,128)(2,1)S(1)}, u32[]{:S(2)}, u32[]{:S(2)}) collective-permute-start(bf16[2,128,256]{2,1,0:T(8,128)(2,1)S(1)} %bitcast_dynamic-update-slice_fusion.4), channel_id=1, source_target_pairs={{0,1},{1,0},{2,3},{3,2},{4,5},{5,4},{6,7},{7,6},{8,9},{9,8},{10,11... | collective-permute-start | bytes 393224 | tf_op jit(solution)/shard_map/ppermute | solution.py:18
  8.5 8.4 %copy-start.25 = (bf16[1,256,256]{2,1,0:T(8,128)(2,1)S(1)}, bf16[1,256,256]{2,1,0:T(8,128)(2,1)}, u32[]{:S(2)}) copy-start(bf16[1,256,256]{2,1,0:T(8,128)(2,1)} %param.10) | copy-start | bytes 393220
  9.4 32.8 %collective-permute-start.3 = (bf16[2,128,256]{2,1,0:T(8,128)(2,1)S(1)}, bf16[2,128,256]{2,1,0:T(8,128)(2,1)S(1)}, u32[]{:S(2)}, u32[]{:S(2)}) collective-permute-start(bf16[2,128,256]{2,1,0:T(8,128)(2,1)S(1)} %bitcast_dynamic-update-slice_fusion.2), channel_id=1, source_target_pairs={{0,1},{1,0},{2,3},{3,2},{4,5},{5,4},{6,7},{7,6},{8,9},{9,8},{10,11... | collective-permute-start | bytes 393224 | tf_op jit(solution)/shard_map/ppermute | solution.py:18
  11.9 27.5 %collective-permute-start.6 = (bf16[2,128,256]{2,1,0:T(8,128)(2,1)S(1)}, bf16[2,128,256]{2,1,0:T(8,128)(2,1)S(1)}, u32[]{:S(2)}, u32[]{:S(2)}) collective-permute-start(bf16[2,128,256]{2,1,0:T(8,128)(2,1)S(1)} %bitcast_dynamic-update-slice_fusion), channel_id=1, source_target_pairs={{0,1},{1,0},{2,3},{3,2},{4,5},{5,4},{6,7},{7,6},{8,9},{9,8},{10,11... | collective-permute-start | bytes 393224 | tf_op jit(solution)/shard_map/ppermute | solution.py:18
  13.0 8.3 %copy-start.57 = (s32[2,2]{1,0:T(2,128)}, s32[2,2]{1,0:T(2,128)S(1)}, u32[]{:S(2)}) copy-start(s32[2,2]{1,0:T(2,128)S(1)} %iota_clamp_fusion) | copy-start | bytes 52
  13.1 8.6 %copy-start.51 = (f32[2,2]{1,0:T(2,128)}, f32[2,2]{1,0:T(2,128)S(1)}, u32[]{:S(2)}) copy-start(f32[2,2]{1,0:T(2,128)S(1)} %and_convert_fusion.8) | copy-start | bytes 52
  24.9 5.4 %copy-start.42 = (s32[2,1]{1,0:T(2,128)S(1)}, s32[2,1]{1,0:T(2,128)}, u32[]{:S(2)}) copy-start(s32[2,1]{1,0:T(2,128)} %get-tuple-element.179) | copy-start | bytes 28
  24.9 5.4 %copy-start.43 = (s32[2,1]{1,0:T(2,128)S(1)}, s32[2,1]{1,0:T(2,128)}, u32[]{:S(2)}) copy-start(s32[2,1]{1,0:T(2,128)} %get-tuple-element.180) | copy-start | bytes 28
  24.9 5.5 %copy-start.40 = (s32[2,1]{1,0:T(2,128)S(1)}, s32[2,1]{1,0:T(2,128)}, u32[]{:S(2)}) copy-start(s32[2,1]{1,0:T(2,128)} %get-tuple-element.176) | copy-start | bytes 28
  24.9 5.5 %copy-start.41 = (s32[2,1]{1,0:T(2,128)S(1)}, s32[2,1]{1,0:T(2,128)}, u32[]{:S(2)}) copy-start(s32[2,1]{1,0:T(2,128)} %get-tuple-element.177) | copy-start | bytes 28
  24.9 5.6 %copy-start.38 = (s32[2,1]{1,0:T(2,128)S(1)}, s32[2,1]{1,0:T(2,128)}, u32[]{:S(2)}) copy-start(s32[2,1]{1,0:T(2,128)} %get-tuple-element.119) | copy-start | bytes 28
  25.0 5.6 %copy-start.39 = (s32[2,1]{1,0:T(2,128)S(1)}, s32[2,1]{1,0:T(2,128)}, u32[]{:S(2)}) copy-start(s32[2,1]{1,0:T(2,128)} %get-tuple-element.120) | copy-start | bytes 28
  25.0 5.7 %copy-start.33 = (s32[2]{0:T(128)S(1)}, s32[2]{0:T(128)}, u32[]{:S(2)}) copy-start(s32[2]{0:T(128)} %copy-done.32) | copy-start | bytes 28
  25.0 5.7 %copy-start.35 = (s32[2]{0:T(128)S(1)}, s32[2]{0:T(128)}, u32[]{:S(2)}) copy-start(s32[2]{0:T(128)} %copy-done.34) | copy-start | bytes 28
  25.0 6.4 %copy-start.29 = (s32[2]{0:T(128)S(1)}, s32[2]{0:T(128)}, u32[]{:S(2)}) copy-start(s32[2]{0:T(128)} %copy-done.28) | copy-start | bytes 28
  25.0 6.4 %copy-start.31 = (s32[2]{0:T(128)S(1)}, s32[2]{0:T(128)}, u32[]{:S(2)}) copy-start(s32[2]{0:T(128)} %copy-done.30) | copy-start | bytes 28
  25.3 6.8 %copy-start.62 = (f32[2,1,128]{2,1,0:T(1,128)S(1)}, f32[2,1,128]{2,1,0:T(1,128)}, u32[]{:S(2)}) copy-start(f32[2,1,128]{2,1,0:T(1,128)} %fusion.197) | copy-start | bytes 3076
  33.1 12.7 %copy-start.61 = (f32[2,1,128]{2,1,0:T(1,128)S(1)}, f32[2,1,128]{2,1,0:T(1,128)}, u32[]{:S(2)}) copy-start(f32[2,1,128]{2,1,0:T(1,128)} %fusion.187) | copy-start | bytes 3076
  34.7 10.9 %collective-permute-start.2 = (bf16[2,256,256]{2,1,0:T(8,128)(2,1)S(1)}, bf16[2,256,256]{2,1,0:T(8,128)(2,1)S(1)}, u32[]{:S(2)}, u32[]{:S(2)}) collective-permute-start(bf16[2,256,256]{2,1,0:T(8,128)(2,1)S(1)} %maximum_select_fusion.7), channel_id=1, source_target_pairs={{0,2},{2,0},{1,3},{3,1},{4,6},{6,4},{5,7},{7,5},{8,10},{10,8},{9,1... | collective-permute-start | bytes 786440 | tf_op jit(solution)/shard_map/ppermute | solution.py:18
  38.9 58.9 %collective-permute-start.10 = (bf16[2,128,256]{2,1,0:T(8,128)(2,1)}, bf16[2,128,256]{2,1,0:T(8,128)(2,1)}, u32[]{:S(2)}, u32[]{:S(2)}) collective-permute-start(bf16[2,128,256]{2,1,0:T(8,128)(2,1)} %fusion.67), channel_id=1, source_target_pairs={{0,1},{1,0},{2,3},{3,2},{4,5},{5,4},{6,7},{7,6},{8,9},{9,8},{10,11... | collective-permute-start | bytes 393224 | tf_op jit(solution)/shard_map/ppermute | solution.py:18
  40.3 26.1 %collective-permute-start.7 = (bf16[2,256,256]{2,1,0:T(8,128)(2,1)}, bf16[2,256,256]{2,1,0:T(8,128)(2,1)}, u32[]{:S(2)}, u32[]{:S(2)}) collective-permute-start(bf16[2,256,256]{2,1,0:T(8,128)(2,1)} %maximum_select_fusion.9), channel_id=1, source_target_pairs={{0,2},{2,0},{1,3},{3,1},{4,6},{6,4},{5,7},{7,5},{8,10},{10,8},{9,1... | collective-permute-start | bytes 786440 | tf_op jit(solution)/shard_map/ppermute | solution.py:18
  43.1 14.2 %collective-permute-start.4 = (bf16[2,256,256]{2,1,0:T(8,128)(2,1)}, bf16[2,256,256]{2,1,0:T(8,128)(2,1)}, u32[]{:S(2)}, u32[]{:S(2)}) collective-permute-start(bf16[2,256,256]{2,1,0:T(8,128)(2,1)} %maximum_select_fusion.8), channel_id=1, source_target_pairs={{0,2},{2,0},{1,3},{3,1},{4,6},{6,4},{5,7},{7,5},{8,10},{10,8},{9,1... | collective-permute-start | bytes 786440 | tf_op jit(solution)/shard_map/ppermute | solution.py:18
  58.6 14.8 %collective-permute-start.5 = (bf16[2,512,256]{2,1,0:T(8,128)(2,1)S(1)}, bf16[2,512,256]{2,1,0:T(8,128)(2,1)}, u32[]{:S(2)}, u32[]{:S(2)}) collective-permute-start(bf16[2,512,256]{2,1,0:T(8,128)(2,1)S(1)} %maximum_select_fusion.4), channel_id=1, source_target_pairs={{0,4},{4,0},{1,5},{5,1},{2,6},{6,2},{3,7},{7,3},{8,12},{12,8},{9,1... | collective-permute-start | bytes 1572872 | tf_op jit(solution)/shard_map/ppermute | solution.py:18
  62.5 12.3 %copy-start.19 = (bf16[2,1,16384]{2,0,1:T(2,128)(2,1)S(1)}, bf16[2,1,16384]{2,0,1:T(2,128)(2,1)}, u32[]{:S(2)}) copy-start(bf16[2,1,16384]{2,0,1:T(2,128)(2,1)} %copy.384) | copy-start | bytes 196612
  62.5 12.3 %copy-start.27 = (f32[1,2,8,128]{3,1,2,0:T(2,128)S(1)}, f32[1,2,8,128]{3,1,2,0:T(2,128)}, u32[]{:S(2)}) copy-start(f32[1,2,8,128]{3,1,2,0:T(2,128)} %copy.393) | copy-start | bytes 24580
  62.5 12.3 %copy-start.50 = (f32[2]{0:T(128)S(1)}, f32[2]{0:T(128)}, u32[]{:S(2)}) copy-start(f32[2]{0:T(128)} %copy-done.49) | copy-start | bytes 28
  62.5 12.3 %copy-start.60 = (f32[2,1,128]{2,1,0:T(1,128)S(1)}, f32[2,1,128]{2,1,0:T(1,128)}, u32[]{:S(2)}) copy-start(f32[2,1,128]{2,1,0:T(1,128)} %fusion.177) | copy-start | bytes 3076
  63.3 36.3 %collective-permute-start.11 = (bf16[2,256,256]{2,1,0:T(8,128)(2,1)}, bf16[2,256,256]{2,1,0:T(8,128)(2,1)}, u32[]{:S(2)}, u32[]{:S(2)}) collective-permute-start(bf16[2,256,256]{2,1,0:T(8,128)(2,1)} %fusion.49), channel_id=1, source_target_pairs={{0,2},{2,0},{1,3},{3,1},{4,6},{6,4},{5,7},{7,5},{8,10},{10,8},{9,1... | collective-permute-start | bytes 786440 | tf_op jit(solution)/shard_map/ppermute | solution.py:18
  68.5 23.8 %collective-permute-start.8 = (bf16[2,512,256]{2,1,0:T(8,128)(2,1)}, bf16[2,512,256]{2,1,0:T(8,128)(2,1)}, u32[]{:S(2)}, u32[]{:S(2)}) collective-permute-start(bf16[2,512,256]{2,1,0:T(8,128)(2,1)} %maximum_select_fusion.5), channel_id=1, source_target_pairs={{0,4},{4,0},{1,5},{5,1},{2,6},{6,2},{3,7},{7,3},{8,12},{12,8},{9,1... | collective-permute-start | bytes 1572872 | tf_op jit(solution)/shard_map/ppermute | solution.py:18
  89.4 8.3 %copy-start.6 = (f32[2,256,256]{2,1,0:T(8,128)S(1)}, f32[2,256,256]{2,1,0:T(8,128)}, u32[]{:S(2)}) copy-start(f32[2,256,256]{2,1,0:T(8,128)} %copy-done.5) | copy-start | bytes 1572868
  89.6 15.5 %collective-permute-start.13 = (bf16[2,512,256]{2,1,0:T(8,128)(2,1)S(1)}, bf16[2,512,256]{2,1,0:T(8,128)(2,1)S(1)}, u32[]{:S(2)}, u32[]{:S(2)}) collective-permute-start(bf16[2,512,256]{2,1,0:T(8,128)(2,1)S(1)} %fusion.42), channel_id=1, source_target_pairs={{0,4},{4,0},{1,5},{5,1},{2,6},{6,2},{3,7},{7,3},{8,12},{12,8},{9,1... | collective-permute-start | bytes 1572872 | tf_op jit(solution)/shard_map/ppermute | solution.py:18
  94.0 29.7 %collective-permute-start.9 = (bf16[2,1024,256]{2,1,0:T(8,128)(2,1)S(1)}, bf16[2,1024,256]{2,1,0:T(8,128)(2,1)S(1)}, u32[]{:S(2)}, u32[]{:S(2)}) collective-permute-start(bf16[2,1024,256]{2,1,0:T(8,128)(2,1)S(1)} %maximum_select_fusion.2), channel_id=1, source_target_pairs={{0,8},{8,0},{1,9},{9,1},{2,10},{10,2},{3,11},{11,3},{4,12},{12,4},... | collective-permute-start | bytes 3145736 | tf_op jit(solution)/shard_map/ppermute | solution.py:18
  101.4 60.6 %collective-permute-start.12 = (bf16[2,128,256]{2,1,0:T(8,128)(2,1)}, bf16[2,128,256]{2,1,0:T(8,128)(2,1)}, u32[]{:S(2)}, u32[]{:S(2)}) collective-permute-start(bf16[2,128,256]{2,1,0:T(8,128)(2,1)} %fusion.68), channel_id=1, source_target_pairs={{0,1},{1,0},{2,3},{3,2},{4,5},{5,4},{6,7},{7,6},{8,9},{9,8},{10,11... | collective-permute-start | bytes 393224 | tf_op jit(solution)/shard_map/ppermute | solution.py:18
  105.3 19.0 %copy-start.18 = (bf16[2,1,16384]{2,0,1:T(2,128)(2,1)S(1)}, bf16[2,1,16384]{2,0,1:T(2,128)(2,1)}, u32[]{:S(2)}) copy-start(bf16[2,1,16384]{2,0,1:T(2,128)(2,1)} %copy.388) | copy-start | bytes 196612
  105.3 19.0 %copy-start.48 = (f32[2]{0:T(128)S(1)}, f32[2]{0:T(128)}, u32[]{:S(2)}) copy-start(f32[2]{0:T(128)} %copy-done.47) | copy-start | bytes 28
  105.4 19.0 %copy-start.59 = (f32[2,1,128]{2,1,0:T(1,128)S(1)}, f32[2,1,128]{2,1,0:T(1,128)}, u32[]{:S(2)}) copy-start(f32[2,1,128]{2,1,0:T(1,128)} %fusion.167) | copy-start | bytes 3076
  156.4 5.6 %copy-start.8 = (f32[2,256,256]{2,1,0:T(8,128)S(1)}, f32[2,256,256]{2,1,0:T(8,128)}, u32[]{:S(2)}) copy-start(f32[2,256,256]{2,1,0:T(8,128)} %copy-done.7) | copy-start | bytes 1572868
  158.3 24.5 %collective-permute-start.16 = (bf16[2,1024,256]{2,1,0:T(8,128)(2,1)S(1)}, bf16[2,1024,256]{2,1,0:T(8,128)(2,1)S(1)}, u32[]{:S(2)}, u32[]{:S(2)}) collective-permute-start(bf16[2,1024,256]{2,1,0:T(8,128)(2,1)S(1)} %fusion.36), channel_id=1, source_target_pairs={{0,8},{8,0},{1,9},{9,1},{2,10},{10,2},{3,11},{11,3},{4,12},{12,4},... | collective-permute-start | bytes 3145736 | tf_op jit(solution)/shard_map/ppermute | solution.py:18
  158.5 8.8 %collective-permute-start.14 = (bf16[2,256,256]{2,1,0:T(8,128)(2,1)S(1)}, bf16[2,256,256]{2,1,0:T(8,128)(2,1)S(1)}, u32[]{:S(2)}, u32[]{:S(2)}) collective-permute-start(bf16[2,256,256]{2,1,0:T(8,128)(2,1)S(1)} %fusion.50), channel_id=1, source_target_pairs={{0,2},{2,0},{1,3},{3,1},{4,6},{6,4},{5,7},{7,5},{8,10},{10,8},{9,1... | collective-permute-start | bytes 786440 | tf_op jit(solution)/shard_map/ppermute | solution.py:18
  161.8 21.0 %copy-start = (f32[2,1,1024,256]{3,2,0,1:T(8,128)S(1)}, f32[2,1,1024,256]{3,2,0,1:T(8,128)}, u32[]{:S(2)}) copy-start(f32[2,1,1024,256]{3,2,0,1:T(8,128)} %copy.158) | copy-start | bytes 6291460
  167.4 16.4 %copy-start.12 = (bf16[2,1024,256]{2,1,0:T(8,128)(2,1)S(1)}, bf16[2,1024,256]{2,1,0:T(8,128)(2,1)}, u32[]{:S(2)}) copy-start(bf16[2,1024,256]{2,1,0:T(8,128)(2,1)} %copy-done.11) | copy-start | bytes 3145732
  167.4 16.4 %copy-start.16 = (bf16[2,128,1024]{2,1,0:T(8,128)(2,1)S(1)}, bf16[2,128,1024]{2,1,0:T(8,128)(2,1)}, u32[]{:S(2)}) copy-start(bf16[2,128,1024]{2,1,0:T(8,128)(2,1)} %copy-done.15) | copy-start | bytes 1572868
  167.4 16.8 %collective-permute-start.15 = (bf16[2,128,256]{2,1,0:T(8,128)(2,1)S(1)}, bf16[2,128,256]{2,1,0:T(8,128)(2,1)S(1)}, u32[]{:S(2)}, u32[]{:S(2)}) collective-permute-start(bf16[2,128,256]{2,1,0:T(8,128)(2,1)S(1)} %fusion.69), channel_id=1, source_target_pairs={{0,1},{1,0},{2,3},{3,2},{4,5},{5,4},{6,7},{7,6},{8,9},{9,8},{10,11... | collective-permute-start | bytes 393224 | tf_op jit(solution)/shard_map/ppermute | solution.py:18
  183.3 9.3 %collective-permute-start.17 = (bf16[2,512,256]{2,1,0:T(8,128)(2,1)S(1)}, bf16[2,512,256]{2,1,0:T(8,128)(2,1)S(1)}, u32[]{:S(2)}, u32[]{:S(2)}) collective-permute-start(bf16[2,512,256]{2,1,0:T(8,128)(2,1)S(1)} %fusion.43), channel_id=1, source_target_pairs={{0,4},{4,0},{1,5},{5,1},{2,6},{6,2},{3,7},{7,3},{8,12},{12,8},{9,1... | collective-permute-start | bytes 1572872 | tf_op jit(solution)/shard_map/ppermute | solution.py:18
  185.6 11.7 %copy-start.20 = (f32[2,2,16384]{2,1,0:T(2,128)S(1)}, f32[2,2,16384]{2,1,0:T(2,128)}, u32[]{:S(2)}) copy-start(f32[2,2,16384]{2,1,0:T(2,128)} %reshape_reshape_transpose.2) | copy-start | bytes 786436
  185.6 11.7 %copy-start.26 = (f32[1,2,128,128]{3,1,2,0:T(2,128)S(1)}, f32[1,2,128,128]{3,1,2,0:T(2,128)}, u32[]{:S(2)}) copy-start(f32[1,2,128,128]{3,1,2,0:T(2,128)} %copy.373) | copy-start | bytes 393220
  185.6 11.7 %copy-start.52 = (f32[2,2]{1,0:T(2,128)S(1)}, f32[2,2]{1,0:T(2,128)}, u32[]{:S(2)}) copy-start(f32[2,2]{1,0:T(2,128)} %copy-done.51) | copy-start | bytes 52
  185.6 11.7 %copy-start.53 = (f32[2,2]{1,0:T(2,128)S(1)}, f32[2,2]{1,0:T(2,128)}, u32[]{:S(2)}) copy-start(f32[2,2]{1,0:T(2,128)} %get-tuple-element.207) | copy-start | bytes 52
  185.6 11.7 %copy-start.54 = (f32[2,2]{1,0:T(2,128)S(1)}, f32[2,2]{1,0:T(2,128)}, u32[]{:S(2)}) copy-start(f32[2,2]{1,0:T(2,128)} %get-tuple-element.208) | copy-start | bytes 52
  185.6 11.7 %copy-start.55 = (f32[2,2]{1,0:T(2,128)S(1)}, f32[2,2]{1,0:T(2,128)}, u32[]{:S(2)}) copy-start(f32[2,2]{1,0:T(2,128)} %get-tuple-element.203) | copy-start | bytes 52
  185.6 11.7 %copy-start.56 = (f32[2,2]{1,0:T(2,128)S(1)}, f32[2,2]{1,0:T(2,128)}, u32[]{:S(2)}) copy-start(f32[2,2]{1,0:T(2,128)} %get-tuple-element.204) | copy-start | bytes 52
  185.6 11.7 %copy-start.58 = (s32[2,2]{1,0:T(2,128)S(1)}, s32[2,2]{1,0:T(2,128)}, u32[]{:S(2)}) copy-start(s32[2,2]{1,0:T(2,128)} %copy-done.57) | copy-start | bytes 52
  193.5 55.1 %collective-permute-start.18 = (bf16[2,256,256]{2,1,0:T(8,128)(2,1)}, bf16[2,256,256]{2,1,0:T(8,128)(2,1)S(1)}, u32[]{:S(2)}, u32[]{:S(2)}) collective-permute-start(bf16[2,256,256]{2,1,0:T(8,128)(2,1)} %fusion.51), channel_id=1, source_target_pairs={{0,2},{2,0},{1,3},{3,1},{4,6},{6,4},{5,7},{7,5},{8,10},{10,8},{9,1... | collective-permute-start | bytes 786440 | tf_op jit(solution)/shard_map/ppermute | solution.py:18
  198.6 51.5 %copy-start.37 = (f32[256]{0:T(256)S(1)}, f32[256]{0:T(256)}, u32[]{:S(2)}) copy-start(f32[256]{0:T(256)} %param.13) | copy-start | bytes 3076
  199.3 54.7 %copy-start.17 = (f32[2,2,32768]{2,1,0:T(2,128)S(1)}, f32[2,2,32768]{2,1,0:T(2,128)}, u32[]{:S(2)}) copy-start(f32[2,2,32768]{2,1,0:T(2,128)} %reshape.1667) | copy-start | bytes 1572868
  199.3 54.7 %copy-start.21 = (f32[1,2,128,256]{3,1,2,0:T(2,128)S(1)}, f32[1,2,128,256]{3,1,2,0:T(2,128)}, u32[]{:S(2)}) copy-start(f32[1,2,128,256]{3,1,2,0:T(2,128)} %copy.191) | copy-start | bytes 786436
  199.3 54.7 %copy-start.22 = (f32[1,2,128,256]{3,1,2,0:T(2,128)S(1)}, f32[1,2,128,256]{3,1,2,0:T(2,128)}, u32[]{:S(2)}) copy-start(f32[1,2,128,256]{3,1,2,0:T(2,128)} %copy.192) | copy-start | bytes 786436
  248.8 5.0 %collective-permute-start.19 = (bf16[2,128,256]{2,1,0:T(8,128)(2,1)S(1)}, bf16[2,128,256]{2,1,0:T(8,128)(2,1)S(1)}, u32[]{:S(2)}, u32[]{:S(2)}) collective-permute-start(bf16[2,128,256]{2,1,0:T(8,128)(2,1)S(1)} %fusion.70), channel_id=1, source_target_pairs={{0,1},{1,0},{2,3},{3,2},{4,5},{5,4},{6,7},{7,6},{8,9},{9,8},{10,11... | collective-permute-start | bytes 393224 | tf_op jit(solution)/shard_map/ppermute | solution.py:18
  (19 other events, 52.2 us)
